TPU v7x, 256 devices: a whole 4x4x8 slice. The times are simulated.
256 devices in a mesh: row: 16 (over x, z_hi, core), col: 16 (over z_lo, y).
Axes of the slice: x: 4, y: 4, z: 8 (z_hi: 2, z_lo: 4; z = z_hi * 4 + z_lo), core: 2. Of those that a mesh axis runs over, the one named last changes fastest.
Arguments:
- diag_coords: int32 [2, 1536], replicated, may hold values from 0 to 32767
- panel_coords: int32 [2, 16, 1536], P(None, 'row', 'col'), may hold values from 0 to 32767
- test_matrix: bfloat16 [16, 1536, 512], P('row', 'col'), may hold values from -6 to 6
- ranks: int32 [16], replicated, may hold values from 64 to 512, as said below
Outputs:
- panel_left: bfloat16 [16, 1536, 512], P('row', 'col')
- update_right: bfloat16 [16, 16, 1536, 512], P('row', 'col')
Inputs may be any that keep to these rules, and one draw needn't show every extreme that they name: ranks[i] is 512 at tile 0 and 64 at the last tile and falls roughly evenly in between, with small random steps.
All inputs are finite; a program needn't handle non-finite values.
Results may differ from a plain program's by a relative error of at most 0.0068.
Values may be sent and summed in bfloat16 or wider, within the bound.
No kernel may reach another device: no remote copies, remote signals or barrier semaphores. Data moves between devices by JAX's collectives and lax.ppermute only.
A program may use at most 192 MiB of HBM per device.

v0:
```python
import jax
import jax.numpy as jnp
from jax import lax
from jax.sharding import PartitionSpec as P

range_length = 409.6
nugget = 0.5
shift_ratio = 0.01


def broadcast(value, axis, root):
    mine = lax.axis_index(axis) == root
    return lax.psum(jnp.where(mine, value, jnp.zeros_like(value)), axis)


def matern(first, second):
    delta_x = (first[0][:, None] - second[0][None, :]).astype(jnp.float32)
    delta_y = (first[1][:, None] - second[1][None, :]).astype(jnp.float32)
    return jnp.exp(-jnp.sqrt(delta_x * delta_x + delta_y * delta_y) / range_length)


def solve_right(factor, sample):
    return jax.scipy.linalg.solve_triangular(factor, sample.T, lower=True).T


def shards(diag_coords, panel_coords, test_matrix, ranks):
    points = diag_coords.shape[1]
    row_tiles = panel_coords.shape[1]
    width = test_matrix.shape[2]
    n_row = lax.axis_size("row")
    n_col = lax.axis_size("col")
    col_tiles = row_tiles * n_row // n_col
    row_index = lax.axis_index("row")
    col_index = lax.axis_index("col")
    cov = matern(diag_coords, diag_coords) + nugget * jnp.eye(points, dtype=jnp.float32)
    is_owner = (row_index == 0) & (col_index == 0)
    lower = lax.cond(is_owner, jnp.linalg.cholesky, jnp.zeros_like, cov)
    lower = broadcast(lower, ("row", "col"), 0)
    columns = jnp.arange(width, dtype=jnp.int32)
    row_ranks = lax.dynamic_slice_in_dim(ranks, row_index * row_tiles, row_tiles)
    row_mask = (columns[None, :] < row_ranks[:, None]).astype(jnp.float32)
    tests_full = lax.all_gather(test_matrix, "col", axis=1, tiled=True)
    tests_rows = tests_full * row_mask.astype(jnp.bfloat16)[:, None, :]
    local_points = panel_coords.reshape(2, -1)
    block = matern(local_points, diag_coords)
    solved = jax.scipy.linalg.solve_triangular(lower, block.T, lower=True).T
    solved = solved.reshape(row_tiles, -1, points)
    sample = jnp.einsum(
        "inm,imr->inr", solved, tests_rows.astype(jnp.float32), precision=lax.Precision.HIGHEST
    )
    gram_part = jnp.einsum("inr,ins->irs", sample, sample, precision=lax.Precision.HIGHEST)
    gram = lax.psum(gram_part, "col")
    trace = jnp.sum(jnp.diagonal(gram, axis1=1, axis2=2), axis=1)
    shift = shift_ratio * trace / row_ranks.astype(jnp.float32)
    extra = shift[:, None] * row_mask + 1.0 - row_mask
    shifted = gram + extra[:, :, None] * jnp.eye(width, dtype=jnp.float32)[None]
    factor = jnp.linalg.cholesky(shifted)
    left = jax.vmap(solve_right)(factor, sample).astype(jnp.bfloat16)
    coeff_part = jnp.einsum(
        "inm,inr->imr", solved, left.astype(jnp.float32), precision=lax.Precision.HIGHEST
    )
    coeff_piece = lax.psum_scatter(coeff_part, "col", scatter_dimension=1, tiled=True).astype(
        jnp.bfloat16
    )
    coeff = lax.all_gather(coeff_piece, "col", axis=1, tiled=True)
    left_full = lax.all_gather(left, "col", axis=1, tiled=True)
    root = col_index * col_tiles // row_tiles
    stacked = jnp.stack([left_full, coeff])
    slab = broadcast(stacked, "row", root)
    offset = col_index * col_tiles % row_tiles
    col_left = slab[0]
    col_coeff = slab[1]
    core = jnp.einsum("inr,jns->ijrs", coeff, col_coeff, preferred_element_type=jnp.float32)
    core = core.astype(jnp.bfloat16)
    update = jnp.einsum("jns,ijrs->ijnr", col_left, core, preferred_element_type=jnp.float32)
    return (left, update.astype(jnp.bfloat16))


def solution(mesh):
    in_specs = (P(), P(None, "row", "col"), P("row", "col", None), P())
    out_specs = (P("row", "col", None), P("row", "col", None, None))
    return jax.shard_map(shards, mesh=mesh, in_specs=in_specs, out_specs=out_specs, check_vma=False)
```

profile of v0, /device:TPU:24, one launch (start us, length us, event | category | flops | bytes accessed | tf_op | source)
XLA Modules:
  0.0 1680.3 jit_solution(12171304196142821972)
XLA Ops:
  8.1 0.8 slice_reduce_fusion.1
  8.9 7.0 subtract_convert_fusion
  15.9 4.3 iota.299
  20.2 4.8 triangular_solve.302
  25.0 4.8 broadcast.804
  29.8 14.6 conditional.1
  29.8 4.8 broadcast.796
  44.4 4.7 broadcast_select_fusion
  51.7 639.4 %all-reduce.6.cloned.1.call-done = f32[1536,1536]{1,0:T(8,128)} async-done(((f32[1536,1536]{1,0:T(8,128)}), f32[1536,1536]{1,0:T(8,128)}) %all-reduce.6.cloned.1.call-update) | async-done | bytes 9437200 | tf_op jit(solution)/shard_map/psum | solution.py:13
  691.1 8.4 fusion.72
  699.4 35.7 %while.2 = (s32[]{:T(128)}, f32[1536,1536]{1,0:T(8,128)}, s32[12,2]{0,1:T(2,128)S(1)}, f32[12,128,128]{2,1,0:T(8,128)S(1)}, s32[]{:T(128)}) while((s32[]{:T(128)}, f32[1536,1536]{1,0:T(8,128)}, s32[12,2]{0,1:T(2,128)S(1)}, f32[12,128,128]{2,1,0:T(8,128)S(1)}, s32[]{:T(128)}) %tuple.143), condition=%wide.while_cond, body=%wide.while_body.sunk | while | flops 2 | bytes 131181 | solution.py:46
  700.1 2.3 bitcast_dynamic-update-slice_fusion.4
  703.1 2.3 bitcast_dynamic-update-slice_fusion.4
  706.1 2.3 bitcast_dynamic-update-slice_fusion.4
  709.0 2.3 bitcast_dynamic-update-slice_fusion.4
  712.0 2.3 bitcast_dynamic-update-slice_fusion.4
  715.0 2.3 bitcast_dynamic-update-slice_fusion.4
  718.0 2.3 bitcast_dynamic-update-slice_fusion.4
  721.0 2.3 bitcast_dynamic-update-slice_fusion.4
  724.0 2.3 bitcast_dynamic-update-slice_fusion.4
  726.9 2.3 bitcast_dynamic-update-slice_fusion.4
  729.9 2.3 bitcast_dynamic-update-slice_fusion.4
  732.9 2.2 bitcast_dynamic-update-slice_fusion.4
  735.2 117.9 %custom-call.130 = f32[12,128,128]{1,2,0:T(8,128)S(1)} custom-call(f32[12,128,128]{2,1,0:T(8,128)S(1)} %get-tuple-element.41), custom_call_target="InvertDiagBlocksLowerTriangular" | custom-call | tf_op jit(solution)/shard_map/jit(_solve_triangular)/triangular_solve | solution.py:46
  853.3 1.1 convolution_subtract_fusion.11
  854.7 1.2 convolution_subtract_fusion.10
  856.2 1.3 convolution_subtract_fusion.14
  857.7 1.3 convolution_subtract_fusion.13
  859.4 1.4 convolution_subtract_fusion.12
  861.1 1.5 convolution_subtract_fusion.9
  862.8 1.6 convolution_subtract_fusion.8
  864.7 1.6 convolution_subtract_fusion.7
  866.6 1.7 convolution_subtract_fusion.6
  868.7 1.8 convolution_subtract_fusion.5
  870.7 1.9 convolution_subtract_fusion.4
  872.9 2.5 fusion.76
  875.4 2.0 convolution_bitcast_fusion.1
  878.2 157.0 %all-reduce.8.cloned.1.call-done = f32[1,512,512]{1,2,0:T(8,128)} async-done(((f32[1,512,512]{1,2,0:T(8,128)}), f32[1,512,512]{1,2,0:T(8,128)}) %all-reduce.8.cloned.1.call-update) | async-done | bytes 1048592 | tf_op jit(solution)/shard_map/psum | solution.py:52
  1035.3 8.6 gather_fusion
  1045.9 1.3 select_add_fusion.1
  1047.5 1.4 fusion.97
  1049.0 11.7 custom-call.131
  1060.8 9.8 custom-call.132
  1071.4 11.7 custom-call.133
  1083.5 10.0 custom-call.134
  1094.4 11.7 custom-call.135
  1106.3 9.8 custom-call.136
  1116.9 11.9 custom-call.137
  1128.9 0.7 compare_reduce_fusion.14
  1134.3 11.3 while.3
  1135.0 1.4 constant_dynamic-slice_fusion.8
  1137.8 1.4 constant_dynamic-slice_fusion.8
  1140.6 1.4 constant_dynamic-slice_fusion.8
  1143.4 1.4 constant_dynamic-slice_fusion.8
  1145.6 40.1 %custom-call.138 = f32[1,4,128,128]{2,3,1,0:T(8,128)S(1)} custom-call(f32[1,4,128,128]{3,2,1,0:T(8,128)} %bitcast.372), custom_call_target="InvertDiagBlocksLowerTriangular" | custom-call | tf_op jit(solution)/shard_map/vmap(jit(_solve_triangular))/triangular_solve | solution.py:23
  1187.3 4.2 convolution_bitcast_fusion
  1192.3 83.5 %reduce-scatter.2.cloned.1.call-done = f32[1,96,512]{2,1,0:T(8,128)} async-done(((f32[1,1536,512]{2,1,0:T(8,128)}), f32[1,96,512]{2,1,0:T(8,128)}) %reduce-scatter.2.cloned.1.call-update) | async-done | bytes 196624 | tf_op jit(solution)/shard_map/reduce_scatter | solution.py:62
  1275.9 1.6 convert_element_type.82
  1277.5 84.0 %all-gather.6.cloned.1.call-done = bf16[1,1536,512]{2,1,0:T(8,128)(2,1)} async-done(((bf16[1,96,512]{2,1,0:T(8,128)(2,1)}), bf16[1,1536,512]{2,1,0:T(8,128)(2,1)}) %all-gather.6.cloned.1.call-update) | async-done | bytes 1572880 | tf_op jit(solution)/shard_map/all_gather | solution.py:66
  1361.5 83.2 %all-gather.8.cloned.1.call-done = bf16[1,1536,512]{2,1,0:T(8,128)(2,1)} async-done(((bf16[1,96,512]{2,1,0:T(8,128)(2,1)}), bf16[1,1536,512]{2,1,0:T(8,128)(2,1)}) %all-gather.8.cloned.1.call-update) | async-done | bytes 1572880 | tf_op jit(solution)/shard_map/all_gather | solution.py:65
  1444.7 4.0 maximum_select_fusion
  1448.7 218.2 %all-reduce.10.cloned.1.call-done = bf16[2,1,1536,512]{3,2,1,0:T(8,128)(2,1)} async-done(((bf16[2,1,1536,512]{3,2,1,0:T(8,128)(2,1)}), bf16[2,1,1536,512]{3,2,1,0:T(8,128)(2,1)}) %all-reduce.10.cloned.1.call-update) | async-done | bytes 3145744 | tf_op jit(solution)/shard_map/psum | solution.py:13
  1666.9 3.8 fusion.73
  1670.7 1.6 copy.29
  (124 shorter events, 28.8 us)
Async XLA Ops:
  8.0 683.1 %all-reduce.6.cloned.1.call-start = ((), (), s32[]{:S(2)}) async-start(), calls=%async_computation.1 | async-start | bytes 18874368 | tf_op jit(solution)/shard_map/psum | solution.py:13
  49.1 0.7 copy-start.2
  49.1 0.7 copy-start.3
  49.1 823.8 %all-gather.4.cloned.1.call-start = ((), (), s32[]{:S(2)}) async-start(), calls=%async_computation.2 | async-start | bytes 1671168 | tf_op jit(solution)/shard_map/all_gather | solution.py:42
  49.7 985.5 %all-reduce.8.cloned.1.call-start = ((), (), s32[]{:S(2)}) async-start(), calls=%async_computation.3 | async-start | bytes 2097152 | tf_op jit(solution)/shard_map/psum | solution.py:52
  872.9 172.3 %copy-start = (f32[1536,96]{0,1:T(8,128)}, f32[1536,96]{0,1:T(8,128)S(1)}, u32[]{:S(2)}) copy-start(f32[1536,96]{0,1:T(8,128)S(1)} %convolution_dynamic-update-slice_fusion.10) | copy-start | bytes 1769476
  877.4 398.4 %reduce-scatter.2.cloned.1.call-start = ((), (), s32[]{:S(2)}) async-start(), calls=%async_computation.5 | async-start | bytes 3342336 | tf_op jit(solution)/shard_map/reduce_scatter | solution.py:62
  1191.5 170.0 %all-gather.6.cloned.1.call-start = ((), (), s32[]{:S(2)}) async-start(), calls=%async_computation.4 | async-start | bytes 1671168 | tf_op jit(solution)/shard_map/all_gather | solution.py:66
  1192.3 252.4 %all-gather.8.cloned.1.call-start = ((), (), s32[]{:S(2)}) async-start(), calls=%async_computation.6 | async-start | bytes 1671168 | tf_op jit(solution)/shard_map/all_gather | solution.py:65
  1277.5 389.4 %all-reduce.10.cloned.1.call-start = ((), (), s32[]{:S(2)}) async-start(), calls=%async_computation.7 | async-start | bytes 6291456 | tf_op jit(solution)/shard_map/psum | solution.py:13
  1444.7 222.2 %copy-start.1 = (bf16[1,1536,512]{2,1,0:T(8,128)(2,1)S(1)}, bf16[1,1536,512]{2,1,0:T(8,128)(2,1)}, u32[]{:S(2)}) copy-start(bf16[1,1536,512]{2,1,0:T(8,128)(2,1)} %all-gather.8.cloned.1.call-done) | copy-start | bytes 4718596
Sparse Core Ops, SparseCore 0:
  49.3 641.7 all-reduce.5
  1448.8 218.0 all-reduce.9
Sparse Core Ops, SparseCore 1:
  51.4 440.1 all-gather.3
  877.5 157.7 all-reduce.7
  1191.6 84.2 reduce-scatter.1
  1278.3 83.2 all-gather.5
  1363.9 80.7 all-gather.7
where the time goes:
time: 1690 us; the launch traced here: 1680 us
  waiting for transfers between devices  1270 us (75%)
  other arithmetic  269 us (16%)
  local copies, waits for them, and re-layouts  78.2 us (5%)
  matrix products  36 us (2%)
  between operations  20.7 us (1%)
    psum x2, waiting for transfers between devices, broadcast(): return lax.psum(jnp.where(mine, value, jnp.zeros_like(value)), axis)  858 us
    psum x1, waiting for transfers between devices, shards(): gram = lax.psum(gram_part, 'col')  157 us
    another operation x3, other arithmetic, shards(): solved = jax.scipy.linalg.solve_triangular(lower, block.T, lower=True).T  126 us
    all_gather x1, waiting for transfers between devices, shards(): left_full = lax.all_gather(left, 'col', axis=1, tiled=True)  84 us
    reduce_scatter x1, waiting for transfers between devices, shards(): lax.psum_scatter(coeff_part, 'col', scatter_dimension=1, tiled=True)  83.5 us
    all_gather x1, waiting for transfers between devices, shards(): coeff = lax.all_gather(coeff_piece, 'col', axis=1, tiled=True)  83.2 us
    another operation x15, other arithmetic, shards(): factor = jnp.linalg.cholesky(shifted)  79.4 us
    another operation x58, local copies, waits for them, and re-layouts  56.4 us
  transfers between devices with their start and end apart: 7, of which 6 were waited for; matrix products, arithmetic and copies ran while one was open for 11% of the time, Pallas kernels for 0%

commit v1 on v0

--- a/solution.py
+++ b/solution.py
@@ -63,7 +63,9 @@
         jnp.bfloat16
     )
     coeff = lax.all_gather(coeff_piece, "col", axis=1, tiled=True)
-    left_full = lax.all_gather(left, "col", axis=1, tiled=True)
+    left_full = jnp.concatenate(
+        lax.all_to_all(jnp.stack([left] * lax.axis_size("col")), "col", 0, 0), axis=1
+    )
     root = col_index * col_tiles // row_tiles
     stacked = jnp.stack([left_full, coeff])
     slab = broadcast(stacked, "row", root)

time: 1690 us -> 1610 us (0.953)
  waiting for transfers between devices: 1270 us -> 1180 us
    all_gather x1 -> x0, waiting for transfers between devices: 84 us -> none  [shards(): left_full = lax.all_gather(left, 'col', axis=1, tiled=True)]
    another operation x58 -> x59, local copies, waits for them, and re-layouts: 56.4 us -> 57.7 us
  transfers between devices with their start and end apart: 7 -> 7, of which waited for: 6 -> 5; matrix products, arithmetic and copies ran while one was open for 11% -> 12% of each run, Pallas kernels for 0% -> 0%
where the time goes in v1:
time: 1610 us; the launch traced here: 1600 us
  waiting for transfers between devices  1180 us (73%)
  other arithmetic  269 us (17%)
  local copies, waits for them, and re-layouts  79.5 us (5%)
  matrix products  35.8 us (2%)
  between operations  20.6 us (1%)
    psum x2, waiting for transfers between devices, broadcast(): return lax.psum(jnp.where(mine, value, jnp.zeros_like(value)), axis)  858 us
    psum x1, waiting for transfers between devices, shards(): gram = lax.psum(gram_part, 'col')  157 us
    another operation x3, other arithmetic, shards(): solved = jax.scipy.linalg.solve_triangular(lower, block.T, lower=True).T  126 us
    all_gather x1, waiting for transfers between devices, shards(): coeff = lax.all_gather(coeff_piece, 'col', axis=1, tiled=True)  80.8 us
    reduce_scatter x1, waiting for transfers between devices, shards(): lax.psum_scatter(coeff_part, 'col', scatter_dimension=1, tiled=True)  79.6 us
    another operation x15, other arithmetic, shards(): factor = jnp.linalg.cholesky(shifted)  79.5 us
    another operation x58, local copies, waits for them, and re-layouts  56.4 us
    another operation x3, other arithmetic, solve_right(): return jax.scipy.linalg.solve_triangular(factor, sample.T, lower=True).T  40.3 us
  transfers between devices with their start and end apart: 7, of which 5 were waited for; matrix products, arithmetic and copies ran while one was open for 12% of the time, Pallas kernels for 0%

profile of v1, /device:TPU:24, one launch (start us, length us, event | category | flops | bytes accessed | tf_op | source)
XLA Modules:
  0.0 1601.6 jit_solution(1971227600865160873)
XLA Ops:
  8.1 0.8 slice_reduce_fusion
  8.9 7.0 subtract_convert_fusion
  15.9 4.3 iota.299
  20.2 4.8 triangular_solve.302
  25.0 4.8 broadcast.807
  29.8 14.1 conditional.1
  29.8 4.8 broadcast.799
  44.0 4.7 broadcast_select_fusion
  51.1 640.0 %all-reduce.6.cloned.1.call-done = f32[1536,1536]{1,0:T(8,128)} async-done(((f32[1536,1536]{1,0:T(8,128)}), f32[1536,1536]{1,0:T(8,128)}) %all-reduce.6.cloned.1.call-update) | async-done | bytes 9437200 | tf_op jit(solution)/shard_map/psum | solution.py:13
  691.1 8.4 fusion.72
  699.5 35.7 %while.2 = (s32[]{:T(128)}, f32[1536,1536]{1,0:T(8,128)}, s32[12,2]{0,1:T(2,128)S(1)}, f32[12,128,128]{2,1,0:T(8,128)S(1)}, s32[]{:T(128)}) while((s32[]{:T(128)}, f32[1536,1536]{1,0:T(8,128)}, s32[12,2]{0,1:T(2,128)S(1)}, f32[12,128,128]{2,1,0:T(8,128)S(1)}, s32[]{:T(128)}) %tuple.146), condition=%wide.while_cond, body=%wide.while_body.sunk | while | flops 2 | bytes 131181 | solution.py:46
  700.2 2.3 bitcast_dynamic-update-slice_fusion.4
  703.1 2.3 bitcast_dynamic-update-slice_fusion.4
  706.1 2.3 bitcast_dynamic-update-slice_fusion.4
  709.1 2.3 bitcast_dynamic-update-slice_fusion.4
  712.1 2.3 bitcast_dynamic-update-slice_fusion.4
  715.1 2.3 bitcast_dynamic-update-slice_fusion.4
  718.1 2.3 bitcast_dynamic-update-slice_fusion.4
  721.0 2.3 bitcast_dynamic-update-slice_fusion.4
  724.0 2.3 bitcast_dynamic-update-slice_fusion.4
  727.0 2.3 bitcast_dynamic-update-slice_fusion.4
  730.0 2.3 bitcast_dynamic-update-slice_fusion.4
  733.0 2.2 bitcast_dynamic-update-slice_fusion.4
  735.2 117.9 %custom-call.130 = f32[12,128,128]{1,2,0:T(8,128)S(1)} custom-call(f32[12,128,128]{2,1,0:T(8,128)S(1)} %get-tuple-element.41), custom_call_target="InvertDiagBlocksLowerTriangular" | custom-call | tf_op jit(solution)/shard_map/jit(_solve_triangular)/triangular_solve | solution.py:46
  853.3 1.1 convolution_subtract_fusion.11
  854.6 1.2 convolution_subtract_fusion.10
  856.0 1.3 convolution_subtract_fusion.14
  857.6 1.3 convolution_subtract_fusion.13
  859.2 1.5 convolution_subtract_fusion.12
  860.9 1.5 convolution_subtract_fusion.9
  862.6 1.6 convolution_subtract_fusion.8
  864.4 1.7 convolution_subtract_fusion.7
  866.3 1.8 convolution_subtract_fusion.6
  868.4 1.8 convolution_subtract_fusion.5
  870.4 2.0 convolution_subtract_fusion.4
  872.7 2.5 fusion.76
  875.1 2.0 convolution_bitcast_fusion.1
  877.9 157.0 %all-reduce.8.cloned.1.call-done = f32[1,512,512]{1,2,0:T(8,128)} async-done(((f32[1,512,512]{1,2,0:T(8,128)}), f32[1,512,512]{1,2,0:T(8,128)}) %all-reduce.8.cloned.1.call-update) | async-done | bytes 1048592 | tf_op jit(solution)/shard_map/psum | solution.py:52
  1034.9 8.6 gather_fusion
  1045.5 1.3 select_add_fusion.1
  1047.2 1.4 fusion.97
  1048.7 11.7 custom-call.131
  1060.4 9.8 custom-call.132
  1071.0 11.7 custom-call.133
  1083.1 10.0 custom-call.134
  1094.1 11.7 custom-call.135
  1105.9 9.8 custom-call.136
  1116.5 11.9 custom-call.137
  1133.9 11.3 while.3
  1134.6 1.4 constant_dynamic-slice_fusion.8
  1137.4 1.4 constant_dynamic-slice_fusion.8
  1140.3 1.4 constant_dynamic-slice_fusion.8
  1143.1 1.4 constant_dynamic-slice_fusion.8
  1145.2 40.1 %custom-call.138 = f32[1,4,128,128]{2,3,1,0:T(8,128)S(1)} custom-call(f32[1,4,128,128]{3,2,1,0:T(8,128)} %bitcast.372), custom_call_target="InvertDiagBlocksLowerTriangular" | custom-call | tf_op jit(solution)/shard_map/vmap(jit(_solve_triangular))/triangular_solve | solution.py:23
  1187.0 4.2 convolution_bitcast_fusion
  1191.8 1.3 stack.8
  1193.1 11.1 all-to-all-start
  1204.3 79.6 %reduce-scatter.2.cloned.1.call-done = f32[1,96,512]{2,1,0:T(8,128)} async-done(((f32[1,1536,512]{2,1,0:T(8,128)}), f32[1,96,512]{2,1,0:T(8,128)}) %reduce-scatter.2.cloned.1.call-update) | async-done | bytes 196624 | tf_op jit(solution)/shard_map/reduce_scatter | solution.py:62
  1283.8 1.6 convert_element_type.85
  1285.5 80.8 %all-gather.5.cloned.1.call-done = bf16[1,1536,512]{2,1,0:T(8,128)(2,1)} async-done(((bf16[1,96,512]{2,1,0:T(8,128)(2,1)}), bf16[1,1536,512]{2,1,0:T(8,128)(2,1)}) %all-gather.5.cloned.1.call-update) | async-done | bytes 1572880 | tf_op jit(solution)/shard_map/all_gather | solution.py:65
  1366.3 3.6 maximum_select_fusion
  1369.9 218.2 %all-reduce.10.cloned.1.call-done = bf16[2,1,1536,512]{3,2,1,0:T(8,128)(2,1)} async-done(((bf16[2,1,1536,512]{3,2,1,0:T(8,128)(2,1)}), bf16[2,1,1536,512]{3,2,1,0:T(8,128)(2,1)}) %all-reduce.10.cloned.1.call-update) | async-done | bytes 3145744 | tf_op jit(solution)/shard_map/psum | solution.py:13
  1588.1 3.8 fusion.73
  1591.9 1.6 copy.41
  (124 shorter events, 28.4 us)
Async XLA Ops:
  8.0 683.1 %all-reduce.6.cloned.1.call-start = ((), (), s32[]{:S(2)}) async-start(), calls=%async_computation.2 | async-start | bytes 18874368 | tf_op jit(solution)/shard_map/psum | solution.py:13
  48.6 0.7 copy-start.2
  48.6 0.7 copy-start.3
  48.7 824.0 %all-gather.3.cloned.1.call-start = ((), (), s32[]{:S(2)}) async-start(), calls=%async_computation.3 | async-start | bytes 1671168 | tf_op jit(solution)/shard_map/all_gather | solution.py:42
  49.2 985.7 %all-reduce.8.cloned.1.call-start = ((), (), s32[]{:S(2)}) async-start(), calls=%async_computation.4 | async-start | bytes 2097152 | tf_op jit(solution)/shard_map/psum | solution.py:52
  872.6 5.3 copy-start
  877.2 406.7 %reduce-scatter.2.cloned.1.call-start = ((), (), s32[]{:S(2)}) async-start(), calls=%async_computation.5 | async-start | bytes 3342336 | tf_op jit(solution)/shard_map/reduce_scatter | solution.py:62
  1193.1 92.4 %all-to-all-start = ((bf16[16,1,96,512]{3,2,1,0:T(8,128)(2,1)}), bf16[16,1,96,512]{3,2,1,0:T(8,128)(2,1)S(1)}, u32[]{:S(2)}, u32[]{:S(2)}) async-start(bf16[16,1,96,512]{3,2,1,0:T(8,128)(2,1)} %stack.8), calls=%async_computation | async-start | bytes 3145728 | tf_op jit(solution)/shard_map/all_to_all | solution.py:67
  1204.2 162.1 %all-gather.5.cloned.1.call-start = ((), (), s32[]{:S(2)}) async-start(), calls=%async_computation.6 | async-start | bytes 1671168 | tf_op jit(solution)/shard_map/all_gather | solution.py:65
  1285.4 302.7 %all-reduce.10.cloned.1.call-start = ((), (), s32[]{:S(2)}) async-start(), calls=%async_computation.7 | async-start | bytes 6291456 | tf_op jit(solution)/shard_map/psum | solution.py:13
  1366.3 221.8 %copy-start.1 = (bf16[1,1536,512]{2,1,0:T(8,128)(2,1)S(1)}, bf16[1,1536,512]{2,1,0:T(8,128)(2,1)}, u32[]{:S(2)}) copy-start(bf16[1,1536,512]{2,1,0:T(8,128)(2,1)} %all-gather.5.cloned.1.call-done) | copy-start | bytes 4718596
Sparse Core Ops, SparseCore 0:
  48.8 642.2 all-reduce.5
  1370.0 218.0 all-reduce.9
Sparse Core Ops, SparseCore 1:
  50.9 440.7 all-gather.2
  877.2 157.6 all-reduce.7
  1191.3 92.5 reduce-scatter.1
  1285.7 80.6 all-gather.4
